TPU v7x, 32 devices: a whole 2x2x4 slice. The times are simulated.
32 devices in a mesh: space: 16 (over z, x, core), sample: 2 (over y).
Axes of the slice: x: 2, y: 2, z: 4, core: 2. Of those that a mesh axis runs over, the one named last changes fastest.
Arguments:
- spectra: float32 [36, 2, 512, 256], P('sample', None, 'space'), may hold values from -6 to 6
- plane_assign: int32 [2, 18], P('sample'), may hold values from 0 to 17, each once within a row
- fine_state: bfloat16 [4, 32, 131072], P('sample', 'space'), may hold values from 0.3984375 to 1.3984375
- partner_state: float32 [4, 4, 2048], P('sample'), may hold values from 0.4 to 1.4
- coarse_state: float32 [32, 4, 2048], P(('space', 'sample')), may hold values from 0.4 to 1.4
- turbine_x: int32 [16], replicated, may hold values from 0 to 31
- turbine_y: int32 [16], replicated, may hold values from 0 to 62
- turbine_z: int32 [16], replicated, may hold values from 0 to 30
- thrust: float32 [16], replicated, may hold values from 0.5 to 2
Outputs:
- fine_field: float32 [4, 32, 131072], P('sample', 'space')
- partner_field: float32 [4, 4, 2048], P('sample')
- coarse_field: float32 [32, 4, 2048], P(('space', 'sample'))
- estimate: float32 [2], replicated
Inputs may be any that keep to these rules, and one draw needn't show every extreme that they name: `plane_assign`: each row is a permutation of 0 to 17.
All inputs are finite; a program needn't handle non-finite values.
Results may differ from a plain program's by a relative error of at most 0.0003.
Values sent between devices are 32-bit elements; how exact they have to be, the bound alone decides.
A program may use at most 128 MiB of HBM per device.

v0:
```python
import math
import jax
import jax.numpy as jnp
from jax import lax
from jax.sharding import PartitionSpec as P

STEPS = 2
ADVECT = 0.3
DIFFUSE = 0.1
RELAX = 0.05
AMPLITUDE = 0.2
HIGHEST = lax.Precision.HIGHEST


def with_halo(cells, sides, width):
    for axis, dim in sides:
        count = lax.axis_size(axis)
        ends = count - 1
        head = lax.slice_in_dim(cells, 0, width, axis=dim)
        tail = lax.slice_in_dim(cells, cells.shape[dim] - width, cells.shape[dim], axis=dim)
        cells = jnp.concatenate(
            [
                lax.ppermute(tail, axis, [(i, (i + 1) % count) for i in range(ends)]),
                cells,
                lax.ppermute(head, axis, [((i + 1) % count, i) for i in range(ends)]),
            ],
            axis=dim,
        )
    return cells


def advance(extended, inflow, resistance):
    upstream = extended[..., :-2, :, :]
    centre = extended[..., 1:-1, :, :]
    downstream = extended[..., 2:, :, :]
    lateral = (
        jnp.roll(centre, 1, -2)
        + jnp.roll(centre, -1, -2)
        + jnp.roll(centre, 1, -1)
        + jnp.roll(centre, -1, -1)
        - 4.0 * centre
    )
    updated = (
        centre
        + ADVECT * (upstream - centre)
        + DIFFUSE * (upstream + downstream - 2.0 * centre)
        + DIFFUSE * lateral
        + RELAX * (inflow[..., None, :, :] - centre)
    )
    return updated / (1.0 + resistance)


def drag_field(
    turbine_x, turbine_y, turbine_z, thrust, first_plane, length, factor, y_count, z_count
):
    block_size = 8 // factor
    planes = first_plane + jnp.arange(length, dtype=jnp.int32)
    along_x = jnp.where(
        (turbine_x // factor)[:, None] == planes[None, :],
        thrust[:, None],
        jnp.zeros_like(thrust)[:, None],
    )
    y_index = jnp.arange(y_count, dtype=jnp.int32)
    z_index = jnp.arange(z_count, dtype=jnp.int32)
    low_y = (turbine_y * block_size)[:, None]
    low_z = (turbine_z * block_size)[:, None]
    cover_y = ((y_index[None, :] >= low_y) & (y_index[None, :] < low_y + 2 * block_size)).astype(
        thrust.dtype
    )
    cover_z = ((z_index[None, :] >= low_z) & (z_index[None, :] < low_z + 2 * block_size)).astype(
        thrust.dtype
    )
    cross_mask = (cover_y[:, :, None] * cover_z[:, None, :]).reshape(
        thrust.shape[0], y_count * z_count
    )
    return jnp.dot(along_x.T, cross_mask, precision=HIGHEST).reshape(length, y_count, z_count)


def restrict(values):
    leading = values.shape[:-2]
    y_count = values.shape[-2]
    z_count = values.shape[-1]
    return values.reshape(leading + (y_count // 8, 8, z_count // 8, 8)).mean(axis=(-3, -1))


def run_whole(velocity, inflow, resistance):
    for step_index in range(STEPS):
        extended = jnp.concatenate(
            [inflow[..., None, :, :], velocity, velocity[..., -1:, :, :]], axis=-3
        )
        velocity = advance(extended, inflow, resistance)
    return velocity


def twiddle(first_index, second_index, period):
    turn_count = first_index[:, None] * second_index[None, :] % period
    phases = 2.0 * math.pi / period * turn_count.astype(jnp.float32)
    return (jnp.cos(phases), jnp.sin(phases))


def shards(
    spectra,
    plane_assign,
    fine_state,
    partner_state,
    coarse_state,
    turbine_x,
    turbine_y,
    turbine_z,
    thrust,
):
    spaces = lax.axis_size("space")
    slab_index = lax.axis_index("space")
    ky_rows = spectra.shape[2]
    total_y = ky_rows * spaces
    total_z = spectra.shape[3]
    coarse_y = total_y // 8
    coarse_z = total_z // 8
    pair_count = fine_state.shape[0]
    slab_planes = fine_state.shape[1]
    norm_scale = 1.0 / math.sqrt(total_y * total_z)
    assignment = plane_assign[0]
    pair_spectra = jnp.take(spectra, assignment[:pair_count], axis=0)
    alone_spectra = jnp.take(spectra, assignment[pair_count:], axis=0)
    z_cells = jnp.arange(total_z, dtype=jnp.int32)
    y_cells = jnp.arange(total_y, dtype=jnp.int32)
    cosine_z, sine_z = twiddle(z_cells, z_cells, total_z)
    z_table = jnp.stack(
        [jnp.concatenate([cosine_z, sine_z], axis=1), jnp.concatenate([-sine_z, cosine_z], axis=1)]
    )
    cosine_y, sine_y = twiddle(y_cells, y_cells, total_y)
    y_table = jnp.stack([cosine_y, -sine_y])
    pair_pq = jnp.einsum("ncks,csj->nkj", pair_spectra, z_table, precision=HIGHEST).reshape(
        pair_count, ky_rows, 2, total_z
    )
    own_ky = slab_index * ky_rows + jnp.arange(ky_rows, dtype=jnp.int32)
    cosine_own, sine_own = twiddle(own_ky, y_cells, total_y)
    y_own = jnp.stack([cosine_own, -sine_own])
    partial_noise = jnp.einsum("nkcz,cky->nyz", pair_pq, y_own, precision=HIGHEST)
    fine_noise = lax.psum(partial_noise, "space") * norm_scale
    alone_pq = jnp.einsum("ncks,csj->nkj", alone_spectra, z_table, precision=HIGHEST)
    gathered_pq = lax.all_to_all(alone_pq, "space", split_axis=0, concat_axis=1, tiled=True)
    full_plane = jnp.einsum(
        "nkcz,cky->nyz", gathered_pq.reshape(-1, total_y, 2, total_z), y_table, precision=HIGHEST
    )
    alone_noise = restrict(full_plane * norm_scale)
    fine_inflow = 1.0 + AMPLITUDE * fine_noise
    last_plane = slab_planes * spaces - 1
    slab_start = slab_index * slab_planes
    velocity = fine_state.astype(jnp.float32).reshape(pair_count, slab_planes, total_y, total_z)
    fine_drag = drag_field(
        turbine_x, turbine_y, turbine_z, thrust, slab_start, slab_planes, 1, total_y, total_z
    )
    for step_index in range(STEPS):
        extended = with_halo(velocity, (("space", 1),), 1)
        start_plane = slab_start - 1
        length = extended.shape[1]
        global_x = start_plane + jnp.arange(length, dtype=jnp.int32)
        inside = jnp.clip(last_plane - start_plane, 0, length - 1)
        edge_plane = lax.dynamic_index_in_dim(extended, inside, axis=1, keepdims=True)
        below_mask = (global_x < 0)[None, :, None, None]
        above_mask = (global_x > last_plane)[None, :, None, None]
        velocity = advance(
            jnp.where(
                below_mask, fine_inflow[:, None], jnp.where(above_mask, edge_plane, extended)
            ),
            fine_inflow,
            fine_drag,
        )
    coarse_planes = slab_planes * spaces // 8
    coarse_drag = drag_field(
        turbine_x, turbine_y, turbine_z, thrust, 0, coarse_planes, 8, coarse_y, coarse_z
    )
    partner_inflow = 1.0 + AMPLITUDE * restrict(fine_noise)
    alone_inflow = 1.0 + AMPLITUDE * alone_noise
    partner = run_whole(
        partner_state.reshape(pair_count, coarse_planes, coarse_y, coarse_z),
        partner_inflow,
        coarse_drag,
    )
    alone_runs = run_whole(
        coarse_state.reshape(-1, coarse_planes, coarse_y, coarse_z), alone_inflow, coarse_drag
    )
    fine_power = jnp.sum(fine_drag * velocity * velocity * velocity, axis=(1, 2, 3)) / 256.0
    partner_power = jnp.sum(coarse_drag * partner * partner * partner, axis=(1, 2, 3)) / 4.0
    alone_power = jnp.sum(coarse_drag * alone_runs * alone_runs * alone_runs, axis=(1, 2, 3)) / 4.0
    leader = (slab_index == 0).astype(jnp.float32)
    partials = jnp.stack(
        [jnp.sum(fine_power) - leader * jnp.sum(partner_power), jnp.sum(alone_power)]
    )
    totals = lax.psum(partials, ("space", "sample"))
    samples_count = lax.axis_size("sample")
    counts = jnp.array(
        [pair_count * samples_count, alone_runs.shape[0] * spaces * samples_count], jnp.float32
    )
    estimate = totals / counts
    fine_field = velocity.reshape(pair_count, slab_planes, total_y * total_z)
    partner_field = partner.reshape(pair_count, coarse_planes, coarse_y * coarse_z)
    coarse_field = alone_runs.reshape(alone_runs.shape[0], coarse_planes, coarse_y * coarse_z)
    return (fine_field, partner_field, coarse_field, estimate)


def solution(mesh):
    placed = (
        P("sample", None, "space", None),
        P("sample", None),
        P("sample", "space", None),
        P("sample", None, None),
        P(("space", "sample"), None, None),
        P(),
        P(),
        P(),
        P(),
    )
    return jax.shard_map(
        shards,
        mesh=mesh,
        in_specs=placed,
        out_specs=(
            P("sample", "space", None),
            P("sample", None, None),
            P(("space", "sample"), None, None),
            P(),
        ),
        check_vma=False,
    )
```

profile of v0, /device:TPU:0, one launch (start us, length us, event | category | flops | bytes accessed | tf_op | source)
XLA Modules:
  0.0 247.3 jit_solution(2681329605193786550)
XLA Ops:
  13.2 2.0 convolution_bitcast_fusion.1
  15.3 1.6 reshape.827
  18.5 3.3 %collective-permute-start = (f32[2,1,512,256]{3,2,1,0:T(8,128)}, f32[2,1,512,256]{3,2,1,0:T(8,128)}, u32[]{:S(2)}, u32[]{:S(2)}) collective-permute-start(f32[2,1,512,256]{3,2,1,0:T(8,128)} %get-tuple-element.29), channel_id=1, source_target_pairs={{0,2},{2,4},{4,6},{6,8},{8,10},{10,12},{12,14},{14,16},{16,18},{18... | collective-permute-start | bytes 3145736 | tf_op jit(solution)/shard_map/ppermute | solution.py:23
  23.2 1.6 gather_fusion.1
  24.8 4.4 %convolution_bitcast_fusion = f32[16,32,512]{2,1,0:T(8,128)} fusion(f32[16,2,32,256]{3,2,1,0:T(8,128)} %gather_fusion.1, f32[1,256,512]{2,1,0:T(8,128)} %copy-done.9, f32[1,256,512]{2,1,0:T(8,128)} %copy-done.8, pred[16]{0:T(512)(128)(4,1)S(1)} %compare_and_fusion), kind=kOutput, calls=%fused_computation.42 | convolution fusion | flops 1611137024 | bytes 3145744 | tf_op jit(solution)/shard_map/ncks,csj->nkj/dot_general | solution.py:141
  29.3 8.4 %all-to-all-start = ((f32[16,32,512]{2,1,0:T(8,128)}), f32[16,32,512]{2,1,0:T(8,128)}, u32[]{:S(2)}, u32[]{:S(2)}) async-start(f32[16,32,512]{2,1,0:T(8,128)} %convolution_bitcast_fusion), calls=%async_computation | async-start | bytes 2097152 | tf_op jit(solution)/shard_map/all_to_all | solution.py:142
  42.3 5.0 %sine_negate_fusion = (f32[1,512,512]{1,2,0:T(8,128)}, f32[1,512,512]{1,2,0:T(8,128)}) fusion(), kind=kLoop, calls=%fused_computation.52 | loop fusion | flops 3932160 | bytes 2097152 | tf_op jit(solution)/shard_map/neg | solution.py:132
  52.2 7.8 %fusion = f32[2,512,256]{2,0,1:T(2,128)S(1)} fusion(f32[16]{0:T(128)S(1)} %copy-done.17, s32[16]{0:T(128)S(1)} %copy-done.22, s32[2]{0:T(128)S(1)} %iota_add_fusion, f32[2,8,512,256]{3,2,1,0:T(8,128)S(1)} %bitcast.72), kind=kOutput, calls=%fused_computation.2 | convolution fusion | flops 50331712 | bytes 9437320 | tf_op jit(solution)/shard_map/dot_general | solution.py:76
  61.6 61.0 %all-reduce.2.cloned.1.call-done = f32[2,512,256]{2,1,0:T(8,128)} async-done(((f32[2,512,256]{2,1,0:T(8,128)}), f32[2,512,256]{2,1,0:T(8,128)}) %all-reduce.2.cloned.1.call-update) | async-done | bytes 1048592 | tf_op jit(solution)/shard_map/psum | solution.py:140
  122.6 2.4 broadcast_multiply_fusion.1
  125.0 12.1 %reshape.818 = f32[2,64,8,32,8]{4,3,2,1,0:T(8,128)} reshape(f32[2,512,256]{2,1,0:T(8,128)} %get-tuple-element.30) | data formatting | bytes 2097152 | tf_op jit(solution)/shard_map/reshape | solution.py:83
  137.1 7.0 %reduce_sum.67 = f32[2,64,32]{2,1,0:T(8,128)S(1)} reduce(f32[2,64,8,32,8]{4,3,2,1,0:T(8,128)} %reshape.818, f32[]{:T(128)} %constant.168.clone.1), dimensions={2,4}, to_apply=%region_1.2 | reduce | flops 258048 | bytes 1064964 | tf_op jit(solution)/shard_map/reduce_sum | solution.py:83
  144.1 1.7 fusion.66
  154.8 2.8 %fusion.15 = f32[2,2,512,256]{3,2,1,0:T(8,128)S(1)} fusion(f32[2,4,512,256]{3,2,1,0:T(8,128)S(1)} %select_select_fusion.1, f32[2,2,511,256]{3,2,1,0:T(8,128)S(1)} %get-tuple-element.23, f32[2,2,1,256]{3,2,1,0:T(1,128)S(1)} %get-tuple-element.25, f32[2,2,1,256]{3,2,1,0:T(1,128)S(1)} %get-tuple-element.24, f32[2,2,511,256]{3,2,1,0:T(8,128)S(1)} %get-tuple-element.22, ...), kind=kLoop, calls=%fused_computation.24 | loop fusion | flops 12058624 | bytes 18874368 | tf_op jit(solution)/shard_map/div | solution.py:50
  160.4 4.0 %collective-permute-start.2 = (f32[2,1,512,256]{3,2,1,0:T(8,128)}, f32[2,1,512,256]{3,2,1,0:T(8,128)}, u32[]{:S(2)}, u32[]{:S(2)}) collective-permute-start(f32[2,1,512,256]{3,2,1,0:T(8,128)} %get-tuple-element.26), channel_id=1, source_target_pairs={{0,2},{2,4},{4,6},{6,8},{8,10},{10,12},{12,14},{14,16},{16,18},{18... | collective-permute-start | bytes 3145736 | tf_op jit(solution)/shard_map/ppermute | solution.py:23
  164.4 2.9 %reshape.822 = f32[512,2,256]{2,1,0:T(2,128)} reshape(f32[16,32,512]{2,1,0:T(8,128)} %all-to-all-done) | data formatting | bytes 2097152 | tf_op jit(solution)/shard_map/reshape.7
  167.3 4.5 %fusion.31 = f32[512,256]{1,0:T(8,128)} fusion(f32[1,512,512]{1,2,0:T(8,128)} %get-tuple-element.84, f32[1,512,512]{1,2,0:T(8,128)} %get-tuple-element.85, f32[512,2,256]{2,1,0:T(2,128)} %reshape.822), kind=kOutput, calls=%fused_computation.45 | convolution fusion | flops 1611268096 | bytes 3670016 | tf_op jit(solution)/shard_map/nkcz,cky->nyz/dot_general | solution.py:143
  171.8 7.1 %reshape.823 = f32[64,8,32,8]{3,2,1,0:T(8,128)} reshape(f32[512,256]{1,0:T(8,128)} %fusion.31) | data formatting | bytes 1048576 | tf_op jit(solution)/shard_map/reshape | solution.py:83
  178.9 4.1 %reduce_sum.68 = f32[64,32]{1,0:T(8,128)S(1)} reduce(f32[64,8,32,8]{3,2,1,0:T(8,128)} %reshape.823, f32[]{:T(128)} %constant.168.clone.1), dimensions={1,3}, to_apply=%region_2.3 | reduce | flops 129024 | bytes 532484 | tf_op jit(solution)/shard_map/reduce_sum | solution.py:83
  186.8 2.0 pad_maximum_fusion
  188.9 2.1 select_select_fusion
  193.7 3.2 %fusion.3 = (f32[2]{0:T(128)S(1)}, f32[2,2,512,256]{3,2,1,0:T(8,128)S(1)}) fusion(f32[2,512,256]{2,1,0:T(8,128)S(1)} %copy-done.10, f32[2,512,256]{2,1,0:T(8,128)S(1)} %copy-done.5, f32[2,512,256]{2,1,0:T(8,128)S(1)} %get-tuple-element.31, f32[2,2,512,1]{3,2,1,0:T(8,128)S(1)} %get-tuple-element.15, f32[2,2,512,255]{3,2,1,0:T(8,128)S(1)} %get-tuple-element.17, ...), kind=kLoop, calls=%fused_computation.10 | loop fusion | flops 14155774 | bytes 19922952 | tf_op jit(solution)/shard_map/reduce_sum | solution.py:184
  198.2 2.4 reshape.816
  200.6 39.4 %psum.15 = f32[2]{0:T(128)S(1)} all-reduce(f32[2]{0:T(128)S(1)} %pad_maximum_fusion.9), channel_id=1, replica_groups=mesh['space'=16,'sample'=2] {'space','sample'}, use_global_device_ids=true, to_apply=%region_8.9 | all-reduce | flops 2 | bytes 16 | tf_op jit(solution)/shard_map/psum | solution.py:191
  (140 shorter events, 37.9 us)
Async XLA Ops:
  7.2 3.8 %copy-start = (f32[18,2,32,256]{3,2,1,0:T(8,128)S(1)}, f32[18,2,32,256]{3,2,1,0:T(8,128)}, u32[]{:S(2)}) copy-start(f32[18,2,32,256]{3,2,1,0:T(8,128)} %param.10) | copy-start | bytes 3538948
  7.2 115.4 %all-reduce.2.cloned.1.call-start = ((), (), s32[]{:S(2)}) async-start(), calls=%async_computation.1 | async-start | bytes 2097152 | tf_op jit(solution)/shard_map/psum | solution.py:140
  16.9 6.2 %copy-start.23 = (s32[1,18]{1,0:T(1,128)S(1)}, s32[1,18]{1,0:T(1,128)}, u32[]{:S(2)}) copy-start(s32[1,18]{1,0:T(1,128)} %param.11) | copy-start | bytes 220
  18.5 130.8 %collective-permute-start = (f32[2,1,512,256]{3,2,1,0:T(8,128)}, f32[2,1,512,256]{3,2,1,0:T(8,128)}, u32[]{:S(2)}, u32[]{:S(2)}) collective-permute-start(f32[2,1,512,256]{3,2,1,0:T(8,128)} %get-tuple-element.29), channel_id=1, source_target_pairs={{0,2},{2,4},{4,6},{6,8},{8,10},{10,12},{12,14},{14,16},{16,18},{18... | collective-permute-start | bytes 3145736 | tf_op jit(solution)/shard_map/ppermute | solution.py:23
  21.8 129.0 %collective-permute-start.1 = (f32[2,1,512,256]{3,2,1,0:T(8,128)}, f32[2,1,512,256]{3,2,1,0:T(8,128)}, u32[]{:S(2)}, u32[]{:S(2)}) collective-permute-start(f32[2,1,512,256]{3,2,1,0:T(8,128)} %get-tuple-element.28), channel_id=1, source_target_pairs={{2,0},{4,2},{6,4},{8,6},{10,8},{12,10},{14,12},{16,14},{18,16},{20... | collective-permute-start | bytes 3145736 | tf_op jit(solution)/shard_map/ppermute | solution.py:25
  24.8 12.8 %copy-start.15 = (f32[2,4,2048]{2,1,0:T(4,128)S(1)}, f32[2,4,2048]{2,1,0:T(4,128)}, u32[]{:S(2)}) copy-start(f32[2,4,2048]{2,1,0:T(4,128)} %param.13) | copy-start | bytes 196612
  29.3 135.2 %all-to-all-start = ((f32[16,32,512]{2,1,0:T(8,128)}), f32[16,32,512]{2,1,0:T(8,128)}, u32[]{:S(2)}, u32[]{:S(2)}) async-start(f32[16,32,512]{2,1,0:T(8,128)} %convolution_bitcast_fusion), calls=%async_computation | async-start | bytes 2097152 | tf_op jit(solution)/shard_map/all_to_all | solution.py:142
  37.6 2.8 %copy-start.20 = (s32[16]{0:T(128)S(1)}, s32[16]{0:T(128)}, u32[]{:S(2)}) copy-start(s32[16]{0:T(128)} %param.17) | copy-start | bytes 196
  37.6 2.8 %copy-start.21 = (s32[16]{0:T(128)S(1)}, s32[16]{0:T(128)}, u32[]{:S(2)}) copy-start(s32[16]{0:T(128)} %param.16) | copy-start | bytes 196
  37.8 3.2 %copy-start.2 = (f32[2,4,64,32]{3,2,1,0:T(8,128)}, f32[2,4,64,32]{3,2,1,0:T(8,128)S(1)}, u32[]{:S(2)}) copy-start(f32[2,4,64,32]{3,2,1,0:T(8,128)S(1)} %reshape.817) | copy-start | bytes 196612
  37.8 3.2 %copy-start.22 = (s32[16]{0:T(128)S(1)}, s32[16]{0:T(128)}, u32[]{:S(2)}) copy-start(s32[16]{0:T(128)} %param.15) | copy-start | bytes 196
  37.8 3.3 %copy-start.17 = (f32[16]{0:T(128)S(1)}, f32[16]{0:T(128)}, u32[]{:S(2)}) copy-start(f32[16]{0:T(128)} %param.18) | copy-start | bytes 196
  40.4 6.9 %copy-start.16 = (f32[1,4,2048]{2,1,0:T(4,128)S(1)}, f32[1,4,2048]{2,1,0:T(4,128)}, u32[]{:S(2)}) copy-start(f32[1,4,2048]{2,1,0:T(4,128)} %param.14) | copy-start | bytes 98308
  41.5 9.3 %copy-start.13 = (f32[4,64,32]{2,1,0:T(8,128)}, f32[4,64,32]{2,1,0:T(8,128)S(1)}, u32[]{:S(2)}) copy-start(f32[4,64,32]{2,1,0:T(8,128)S(1)} %reshape.819) | copy-start | bytes 98308
  47.4 12.7 %copy-start.6 = (f32[1,4,64,32]{3,2,1,0:T(8,128)}, f32[1,4,64,32]{3,2,1,0:T(8,128)S(1)}, u32[]{:S(2)}) copy-start(f32[1,4,64,32]{3,2,1,0:T(8,128)S(1)} %reshape.821) | copy-start | bytes 98308
  137.0 7.1 %copy-start.3 = (f32[2,4,64,32]{3,2,1,0:T(8,128)S(1)}, f32[2,4,64,32]{3,2,1,0:T(8,128)}, u32[]{:S(2)}) copy-start(f32[2,4,64,32]{3,2,1,0:T(8,128)} %copy-done.2) | copy-start | bytes 196612
  137.0 7.1 %slice-start = ((f32[2,4,64,32]{3,2,1,0:T(8,128)}), f32[2,1,64,32]{3,2,1,0:T(8,128)S(1)}, s32[]{:S(2)}) async-start(f32[2,4,64,32]{3,2,1,0:T(8,128)} %copy-done.2), calls=%async_computation.2 | async-start | bytes 131072 | tf_op jit(solution)/shard_map/slice | solution.py:89
  159.1 27.7 %collective-permute-start.3 = (f32[2,1,512,256]{3,2,1,0:T(8,128)}, f32[2,1,512,256]{3,2,1,0:T(8,128)}, u32[]{:S(2)}, u32[]{:S(2)}) collective-permute-start(f32[2,1,512,256]{3,2,1,0:T(8,128)} %get-tuple-element.27), channel_id=1, source_target_pairs={{2,0},{4,2},{6,4},{8,6},{10,8},{12,10},{14,12},{16,14},{18,16},{20... | collective-permute-start | bytes 3145736 | tf_op jit(solution)/shard_map/ppermute | solution.py:25
  160.4 26.4 %collective-permute-start.2 = (f32[2,1,512,256]{3,2,1,0:T(8,128)}, f32[2,1,512,256]{3,2,1,0:T(8,128)}, u32[]{:S(2)}, u32[]{:S(2)}) collective-permute-start(f32[2,1,512,256]{3,2,1,0:T(8,128)} %get-tuple-element.26), channel_id=1, source_target_pairs={{0,2},{2,4},{4,6},{6,8},{8,10},{10,12},{12,14},{14,16},{16,18},{18... | collective-permute-start | bytes 3145736 | tf_op jit(solution)/shard_map/ppermute | solution.py:23
  178.8 4.1 %copy-start.7 = (f32[1,4,64,32]{3,2,1,0:T(8,128)S(1)}, f32[1,4,64,32]{3,2,1,0:T(8,128)}, u32[]{:S(2)}) copy-start(f32[1,4,64,32]{3,2,1,0:T(8,128)} %copy-done.6) | copy-start | bytes 98308
  178.8 4.1 %slice-start.1 = ((f32[1,4,64,32]{3,2,1,0:T(8,128)}), f32[1,1,64,32]{3,2,1,0:T(8,128)S(1)}, s32[]{:S(2)}) async-start(f32[1,4,64,32]{3,2,1,0:T(8,128)} %copy-done.6), calls=%async_computation.3 | async-start | bytes 65536 | tf_op jit(solution)/shard_map/slice | solution.py:89
  178.9 4.1 %copy-start.11 = (f32[1,4,64,32]{3,2,1,0:T(8,128)S(1)}, f32[1,4,64,32]{3,2,1,0:T(8,128)}, u32[]{:S(2)}) copy-start(f32[1,4,64,32]{3,2,1,0:T(8,128)} %reshape.824) | copy-start | bytes 98308
  198.2 42.3 %copy-start.1 = (f32[18,2,32,256]{3,2,1,0:T(8,128)S(1)}, f32[18,2,32,256]{3,2,1,0:T(8,128)}, u32[]{:S(2)}) copy-start(f32[18,2,32,256]{3,2,1,0:T(8,128)} %param.10) | copy-start | bytes 3538948
  198.2 41.8 %copy-start.24 = (f32[2]{0:T(128)S(1)}, f32[2]{0:T(128)}, u32[]{:S(2)}) copy-start(f32[2]{0:T(128)} %constant.181) | copy-start | bytes 28
  (9 other events, 11.1 us)
Sparse Core Ops, SparseCore 0:
  15.4 107.1 all-reduce.1
where the time goes:
time: 248 us; the launch traced here: 247 us
  waiting for transfers between devices  61 us (25%)
  local copies, waits for them, and re-layouts  48.3 us (19%)
  other arithmetic  43.8 us (18%)
  blocking collectives  39.4 us (16%)
  matrix products  19.8 us (8%)
  starting transfers between devices  18.3 us (7%)
  between operations  16.6 us (7%)
    psum x1, waiting for transfers between devices, shards(): fine_noise = lax.psum(partial_noise, 'space') * norm_scale  61 us
    psum x1, blocking collectives, shards(): totals = lax.psum(partials, ('space', 'sample'))  39.4 us
    reshape x2, local copies, waits for them, and re-layouts, restrict(): values.reshape(leading + (y_count // 8, 8, z_count // 8, 8))  19.2 us
    reduce_sum x2, other arithmetic, restrict(): values.reshape(leading + (y_count // 8, 8, z_count // 8, 8))  11.1 us
    all_to_all x1, starting transfers between devices, shards(): lax.all_to_all(alone_pq, 'space', split_axis=0, concat_axis=1, tiled=True)  8.37 us
    dot_general x2, matrix products, drag_field(): jnp.dot(along_x.T, cross_mask, precision=HIGHEST)  8.14 us
    ppermute x2, starting transfers between devices, with_halo(): lax.ppermute(tail, axis, [(i, (i + 1) % count) for i in range(ends)])  7.36 us
    div x3, other arithmetic, advance(): return updated / (1.0 + resistance)  5.88 us
  transfers between devices with their start and end apart: 6, of which 1 were waited for; matrix products, arithmetic and copies ran while one was open for 36% of the time, Pallas kernels for 0%

commit v1 on v0

--- a/solution.py
+++ b/solution.py
@@ -137,7 +137,7 @@
     cosine_own, sine_own = twiddle(own_ky, y_cells, total_y)
     y_own = jnp.stack([cosine_own, -sine_own])
     partial_noise = jnp.einsum("nkcz,cky->nyz", pair_pq, y_own, precision=HIGHEST)
-    fine_noise = lax.psum(partial_noise, "space") * norm_scale
+    fine_noise = jnp.sum(lax.all_gather(partial_noise, "space"), axis=0) * norm_scale
     alone_pq = jnp.einsum("ncks,csj->nkj", alone_spectra, z_table, precision=HIGHEST)
     gathered_pq = lax.all_to_all(alone_pq, "space", split_axis=0, concat_axis=1, tiled=True)
     full_plane = jnp.einsum(

time: 248 us -> 306 us (1.23)
  blocking collectives: 39.4 us -> 57.7 us
  waiting for transfers between devices: 61 us -> 76.7 us
  other arithmetic: 43.8 us -> 56 us
  local copies, waits for them, and re-layouts: 48.3 us -> 56.7 us
    psum x1 -> x0, waiting for transfers between devices: 61 us -> none  [shards(): fine_noise = lax.psum(partial_noise, 'space') * norm_scale]
    all_gather x0 -> x1, waiting for transfers between devices: none -> 58.5 us  [shards(): lax.all_gather(partial_noise, 'space')]
    psum x1, blocking collectives: 39.4 us -> 57.7 us  [shards(): totals = lax.psum(partials, ('space', 'sample'))]
    all_to_all x1, waiting for transfers between devices: 0.01 us -> 18.2 us  [shards(): lax.all_to_all(alone_pq, 'space', split_axis=0, concat_axis=1, tiled=True)]
    reshape x2 -> x1, local copies, waits for them, and re-layouts: 19.2 us -> 7.08 us  [restrict(): values.reshape(leading + (y_count // 8, 8, z_count // 8, 8))]
    mul x0 -> x1, local copies, waits for them, and re-layouts: none -> 11.1 us  [shards(): jnp.sum(lax.all_gather(partial_noise, 'space'), axis=0) * norm_scale]
    reduce_sum x0 -> x1, other arithmetic: none -> 6.98 us  [shards(): jnp.sum(lax.all_gather(partial_noise, 'space'), axis=0) * norm_scale]
    dot_general x2, matrix products: 8.14 us -> 12.7 us  [drag_field(): jnp.dot(along_x.T, cross_mask, precision=HIGHEST)]
  transfers between devices with their start and end apart: 6 -> 6, of which waited for: 1 -> 2; matrix products, arithmetic and copies ran while one was open for 36% -> 21% of each run, Pallas kernels for 0% -> 0%
where the time goes in v1:
time: 306 us; the launch traced here: 305 us
  waiting for transfers between devices  76.7 us (25%)
  blocking collectives  57.7 us (19%)
  local copies, waits for them, and re-layouts  56.7 us (19%)
  other arithmetic  56 us (18%)
  matrix products  22.8 us (7%)
  starting transfers between devices  18.6 us (6%)
  between operations  16.9 us (6%)
    all_gather x1, waiting for transfers between devices, shards(): lax.all_gather(partial_noise, 'space')  58.5 us
    psum x1, blocking collectives, shards(): totals = lax.psum(partials, ('space', 'sample'))  57.7 us
    all_to_all x1, waiting for transfers between devices, shards(): lax.all_to_all(alone_pq, 'space', split_axis=0, concat_axis=1, tiled=True)  18.2 us
    dot_general x2, matrix products, drag_field(): jnp.dot(along_x.T, cross_mask, precision=HIGHEST)  12.7 us
    reduce_sum x2, other arithmetic, restrict(): values.reshape(leading + (y_count // 8, 8, z_count // 8, 8))  11.3 us
    mul x1, local copies, waits for them, and re-layouts, shards(): jnp.sum(lax.all_gather(partial_noise, 'space'), axis=0) * norm_scale  11.1 us
    all_to_all x1, starting transfers between devices, shards(): lax.all_to_all(alone_pq, 'space', split_axis=0, concat_axis=1, tiled=True)  8.49 us
    unnamed x86, local copies, waits for them, and re-layouts  7.89 us
  transfers between devices with their start and end apart: 6, of which 2 were waited for; matrix products, arithmetic and copies ran while one was open for 21% of the time, Pallas kernels for 0%

profile of v1, /device:TPU:0, one launch (start us, length us, event | category | flops | bytes accessed | tf_op | source)
XLA Modules:
  0.0 305.4 jit_solution(9534023889358913570)
XLA Ops:
  18.4 3.4 %collective-permute-start = (f32[2,1,512,256]{3,2,1,0:T(8,128)}, f32[2,1,512,256]{3,2,1,0:T(8,128)}, u32[]{:S(2)}, u32[]{:S(2)}) collective-permute-start(f32[2,1,512,256]{3,2,1,0:T(8,128)} %get-tuple-element.29), channel_id=1, source_target_pairs={{0,2},{2,4},{4,6},{6,8},{8,10},{10,12},{12,14},{14,16},{16,18},{18... | collective-permute-start | bytes 3145736 | tf_op jit(solution)/shard_map/ppermute | solution.py:23
  24.8 4.7 %convolution_bitcast_fusion = f32[16,32,512]{2,1,0:T(8,128)} fusion(f32[16,2,32,256]{3,2,1,0:T(8,128)} %gather_fusion.1, f32[1,256,512]{2,1,0:T(8,128)} %copy-done.12, f32[1,256,512]{2,1,0:T(8,128)} %copy-done.11, pred[16]{0:T(512)(128)(4,1)S(1)} %compare_and_fusion), kind=kOutput, calls=%fused_computation.42 | convolution fusion | flops 1611137024 | bytes 3145744 | tf_op jit(solution)/shard_map/ncks,csj->nkj/dot_general | solution.py:141
  29.5 8.5 %all-to-all-start = ((f32[16,32,512]{2,1,0:T(8,128)}), f32[16,32,512]{2,1,0:T(8,128)}, u32[]{:S(2)}, u32[]{:S(2)}) async-start(f32[16,32,512]{2,1,0:T(8,128)} %convolution_bitcast_fusion), calls=%async_computation | async-start | bytes 2097152 | tf_op jit(solution)/shard_map/all_to_all | solution.py:142
  39.4 5.0 %sine_negate_fusion = (f32[1,512,512]{1,2,0:T(8,128)}, f32[1,512,512]{1,2,0:T(8,128)}) fusion(), kind=kLoop, calls=%fused_computation.52 | loop fusion | flops 3932160 | bytes 2097152 | tf_op jit(solution)/shard_map/neg | solution.py:132
  48.3 4.0 %broadcast_multiply_fusion = f32[16,512,256]{2,1,0:T(8,128)} fusion(f32[16,256]{1,0:T(8,128)S(1)} %fusion.130, f32[16,512]{1,0:T(8,128)S(1)} %fusion.128), kind=kLoop, calls=%fused_computation.7 | loop fusion | flops 2097152 | bytes 8437760 | tf_op jit(solution)/shard_map/mul | solution.py:73
  55.3 12.4 %fusion = f32[2,512,256]{2,0,1:T(2,128)S(1)} fusion(f32[16]{0:T(128)} %param.18, s32[16]{0:T(128)} %param.15, s32[2]{0:T(128)} %iota_add_fusion, f32[2,8,512,256]{3,2,1,0:T(8,128)} %bitcast.73), kind=kOutput, calls=%fused_computation.2 | convolution fusion | flops 50331712 | bytes 9437320 | tf_op jit(solution)/shard_map/dot_general | solution.py:76
  71.9 2.1 copy-done.7
  75.1 18.2 %all-to-all-done = f32[16,32,512]{2,1,0:T(8,128)} async-done(((f32[16,32,512]{2,1,0:T(8,128)}), f32[16,32,512]{2,1,0:T(8,128)}, u32[]{:S(2)}, u32[]{:S(2)}) %all-to-all-start) | async-done | bytes 1048608 | tf_op jit(solution)/shard_map/all_to_all | solution.py:142
  95.1 2.6 fusion.31
  97.7 7.1 %reshape.826 = f32[64,8,32,8]{3,2,1,0:T(8,128)} reshape(f32[512,256]{1,0:T(8,128)} %fusion.31) | data formatting | bytes 1048576 | tf_op jit(solution)/shard_map/reshape | solution.py:83
  104.9 4.1 %reduce_sum.78 = f32[64,32]{1,0:T(8,128)S(1)} reduce(f32[64,8,32,8]{3,2,1,0:T(8,128)} %reshape.826, f32[]{:T(128)} %constant.159.clone.1), dimensions={1,3}, to_apply=%region_2.3 | reduce | flops 129024 | bytes 532484 | tf_op jit(solution)/shard_map/reduce_sum | solution.py:83
  111.7 58.5 %all-gather.3.cloned.1.call-done = f32[32,512,256]{2,1,0:T(8,128)} async-done(((f32[2,512,256]{2,1,0:T(8,128)}), f32[32,512,256]{2,1,0:T(8,128)}) %all-gather.3.cloned.1.call-update) | async-done | bytes 16777232 | tf_op jit(solution)/shard_map/all_gather | solution.py:140
  170.3 7.0 %reduce_sum.76 = f32[2,512,256]{2,1,0:T(8,128)S(1)} reduce(f32[16,2,512,256]{3,2,1,0:T(8,128)} %bitcast.74, f32[]{:T(128)} %constant.159.clone.1), dimensions={0}, to_apply=%region_0.1 | reduce | flops 3932160 | bytes 17825796 | tf_op jit(solution)/shard_map/reduce_sum | solution.py:140
  178.5 2.8 select_select_fusion.1
  181.3 2.5 fusion.169
  183.9 2.8 fusion.167
  188.4 11.1 %mul.452 = f32[2,64,8,32,8]{4,3,2,1,0:T(8,128)} reshape(f32[2,512,256]{2,1,0:T(8,128)S(1)} %get-tuple-element.30) | data formatting | bytes 2097152 | tf_op jit(solution)/shard_map/mul | solution.py:140
  199.6 7.1 %reduce_sum.77 = f32[2,64,32]{2,1,0:T(8,128)S(1)} reduce(f32[2,64,8,32,8]{4,3,2,1,0:T(8,128)} %mul.452, f32[]{:T(128)} %constant.159.clone.1), dimensions={2,4}, to_apply=%region_1.2 | reduce | flops 258048 | bytes 1064964 | tf_op jit(solution)/shard_map/reduce_sum | solution.py:83
  208.6 6.5 %fusion.15 = f32[2,2,512,256]{3,2,1,0:T(8,128)S(1)} fusion(f32[2,4,512,256]{3,2,1,0:T(8,128)} %copy-done.2, f32[2,2,511,256]{3,2,1,0:T(8,128)} %get-tuple-element.23, f32[2,2,1,256]{3,2,1,0:T(1,128)S(1)} %get-tuple-element.25, f32[2,2,1,256]{3,2,1,0:T(1,128)S(1)} %get-tuple-element.24, f32[2,2,511,256]{3,2,1,0:T(8,128)S(1)} %copy-done.10, ...), kind=kLoop, calls=%fused_computation.24 | loop fusion | flops 12058624 | bytes 18874368 | tf_op jit(solution)/shard_map/div | solution.py:50
  218.1 4.0 %collective-permute-start.2 = (f32[2,1,512,256]{3,2,1,0:T(8,128)}, f32[2,1,512,256]{3,2,1,0:T(8,128)}, u32[]{:S(2)}, u32[]{:S(2)}) collective-permute-start(f32[2,1,512,256]{3,2,1,0:T(8,128)} %get-tuple-element.26), channel_id=1, source_target_pairs={{0,2},{2,4},{4,6},{6,8},{8,10},{10,12},{12,14},{14,16},{16,18},{18... | collective-permute-start | bytes 3145736 | tf_op jit(solution)/shard_map/ppermute | solution.py:23
  228.6 2.1 select_select_fusion
  233.4 3.2 %fusion.3 = (f32[2]{0:T(128)S(1)}, f32[2,2,512,256]{3,2,1,0:T(8,128)S(1)}) fusion(f32[2,512,256]{2,1,0:T(8,128)S(1)} %copy-done.13, f32[2,512,256]{2,1,0:T(8,128)S(1)} %copy-done.6, f32[2,512,256]{2,1,0:T(8,128)S(1)} %get-tuple-element.31, f32[2,2,512,1]{3,2,1,0:T(8,128)S(1)} %get-tuple-element.15, f32[2,2,512,255]{3,2,1,0:T(8,128)S(1)} %get-tuple-element.17, ...), kind=kLoop, calls=%fused_computation.10 | loop fusion | flops 14155774 | bytes 19922952 | tf_op jit(solution)/shard_map/reduce_sum | solution.py:184
  237.9 2.4 reshape.820
  240.3 57.7 %psum.7 = f32[2]{0:T(128)S(1)} all-reduce(f32[2]{0:T(128)S(1)} %pad_maximum_fusion.9), channel_id=1, replica_groups=mesh['space'=16,'sample'=2] {'space','sample'}, use_global_device_ids=true, to_apply=%region_8.9 | all-reduce | flops 2 | bytes 16 | tf_op jit(solution)/shard_map/psum | solution.py:191
  (175 shorter events, 48.7 us)
Async XLA Ops:
  7.2 163.1 %all-gather.3.cloned.1.call-start = ((), (), s32[]{:S(2)}) async-start(), calls=%async_computation.1 | async-start | bytes 17825792 | tf_op jit(solution)/shard_map/all_gather | solution.py:140
  18.4 50.7 %collective-permute-start = (f32[2,1,512,256]{3,2,1,0:T(8,128)}, f32[2,1,512,256]{3,2,1,0:T(8,128)}, u32[]{:S(2)}, u32[]{:S(2)}) collective-permute-start(f32[2,1,512,256]{3,2,1,0:T(8,128)} %get-tuple-element.29), channel_id=1, source_target_pairs={{0,2},{2,4},{4,6},{6,8},{8,10},{10,12},{12,14},{14,16},{16,18},{18... | collective-permute-start | bytes 3145736 | tf_op jit(solution)/shard_map/ppermute | solution.py:23
  21.8 48.8 %collective-permute-start.1 = (f32[2,1,512,256]{3,2,1,0:T(8,128)}, f32[2,1,512,256]{3,2,1,0:T(8,128)}, u32[]{:S(2)}, u32[]{:S(2)}) collective-permute-start(f32[2,1,512,256]{3,2,1,0:T(8,128)} %get-tuple-element.28), channel_id=1, source_target_pairs={{2,0},{4,2},{6,4},{8,6},{10,8},{12,10},{14,12},{16,14},{18,16},{20... | collective-permute-start | bytes 3145736 | tf_op jit(solution)/shard_map/ppermute | solution.py:25
  24.8 13.2 %copy-start.37 = (s32[16]{0:T(128)S(1)}, s32[16]{0:T(128)}, u32[]{:S(2)}) copy-start(s32[16]{0:T(128)} %param.17) | copy-start | bytes 196
  24.8 13.2 %copy-start.38 = (s32[16]{0:T(128)S(1)}, s32[16]{0:T(128)}, u32[]{:S(2)}) copy-start(s32[16]{0:T(128)} %param.16) | copy-start | bytes 196
  29.5 9.2 %copy-start.39 = (s32[16]{0:T(128)S(1)}, s32[16]{0:T(128)}, u32[]{:S(2)}) copy-start(s32[16]{0:T(128)} %param.15) | copy-start | bytes 196
  29.5 9.2 %copy-start.34 = (f32[16]{0:T(128)S(1)}, f32[16]{0:T(128)}, u32[]{:S(2)}) copy-start(f32[16]{0:T(128)} %param.18) | copy-start | bytes 196
  29.5 9.6 %copy-start.32 = (f32[2,4,2048]{2,1,0:T(4,128)S(1)}, f32[2,4,2048]{2,1,0:T(4,128)}, u32[]{:S(2)}) copy-start(f32[2,4,2048]{2,1,0:T(4,128)} %param.13) | copy-start | bytes 196612
  29.5 9.8 %copy-start.33 = (f32[1,4,2048]{2,1,0:T(4,128)S(1)}, f32[1,4,2048]{2,1,0:T(4,128)}, u32[]{:S(2)}) copy-start(f32[1,4,2048]{2,1,0:T(4,128)} %param.14) | copy-start | bytes 98308
  29.5 63.7 %all-to-all-start = ((f32[16,32,512]{2,1,0:T(8,128)}), f32[16,32,512]{2,1,0:T(8,128)}, u32[]{:S(2)}, u32[]{:S(2)}) async-start(f32[16,32,512]{2,1,0:T(8,128)} %convolution_bitcast_fusion), calls=%async_computation | async-start | bytes 2097152 | tf_op jit(solution)/shard_map/all_to_all | solution.py:142
  39.1 8.4 %copy-start.18 = (f32[4,64,32]{2,1,0:T(8,128)}, f32[4,64,32]{2,1,0:T(8,128)S(1)}, u32[]{:S(2)}) copy-start(f32[4,64,32]{2,1,0:T(8,128)S(1)} %reshape.822) | copy-start | bytes 98308
  39.3 15.1 %copy-start.3 = (f32[2,4,64,32]{3,2,1,0:T(8,128)}, f32[2,4,64,32]{3,2,1,0:T(8,128)S(1)}, u32[]{:S(2)}) copy-start(f32[2,4,64,32]{3,2,1,0:T(8,128)S(1)} %reshape.821) | copy-start | bytes 196612
  39.4 15.0 %copy-start.8 = (f32[1,4,64,32]{3,2,1,0:T(8,128)}, f32[1,4,64,32]{3,2,1,0:T(8,128)S(1)}, u32[]{:S(2)}) copy-start(f32[1,4,64,32]{3,2,1,0:T(8,128)S(1)} %reshape.824) | copy-start | bytes 98308
  74.0 21.1 %copy-start.14 = (f32[1,512,512]{1,2,0:T(8,128)S(1)}, f32[1,512,512]{1,2,0:T(8,128)}, u32[]{:S(2)}) copy-start(f32[1,512,512]{1,2,0:T(8,128)} %get-tuple-element.84) | copy-start | bytes 3145732
  74.0 21.1 %copy-start.15 = (f32[1,512,512]{1,2,0:T(8,128)S(1)}, f32[1,512,512]{1,2,0:T(8,128)}, u32[]{:S(2)}) copy-start(f32[1,512,512]{1,2,0:T(8,128)} %get-tuple-element.85) | copy-start | bytes 3145732
  199.5 7.3 %copy-start.21 = (f32[2,4,63,32]{3,2,1,0:T(8,128)S(1)}, f32[2,4,63,32]{3,2,1,0:T(8,128)}, u32[]{:S(2)}) copy-start(f32[2,4,63,32]{3,2,1,0:T(8,128)} %get-tuple-element.47) | copy-start | bytes 193540
  199.5 7.3 %copy-start.22 = (f32[2,4,64,31]{3,2,1,0:T(8,128)S(1)}, f32[2,4,64,31]{3,2,1,0:T(8,128)}, u32[]{:S(2)}) copy-start(f32[2,4,64,31]{3,2,1,0:T(8,128)} %get-tuple-element.42) | copy-start | bytes 190468
  199.5 7.3 %copy-start.23 = (f32[2,4,64,31]{3,2,1,0:T(8,128)S(1)}, f32[2,4,64,31]{3,2,1,0:T(8,128)}, u32[]{:S(2)}) copy-start(f32[2,4,64,31]{3,2,1,0:T(8,128)} %get-tuple-element.43) | copy-start | bytes 190468
  199.6 7.3 %copy-start.24 = (f32[2,4,64,1]{3,2,1,0:T(8,128)S(1)}, f32[2,4,64,1]{3,2,1,0:T(8,128)}, u32[]{:S(2)}) copy-start(f32[2,4,64,1]{3,2,1,0:T(8,128)} %get-tuple-element.44) | copy-start | bytes 6148
  199.6 7.3 %copy-start.25 = (f32[2,4,64,1]{3,2,1,0:T(8,128)S(1)}, f32[2,4,64,1]{3,2,1,0:T(8,128)}, u32[]{:S(2)}) copy-start(f32[2,4,64,1]{3,2,1,0:T(8,128)} %get-tuple-element.45) | copy-start | bytes 6148
  216.7 9.8 %collective-permute-start.3 = (f32[2,1,512,256]{3,2,1,0:T(8,128)}, f32[2,1,512,256]{3,2,1,0:T(8,128)}, u32[]{:S(2)}, u32[]{:S(2)}) collective-permute-start(f32[2,1,512,256]{3,2,1,0:T(8,128)} %get-tuple-element.27), channel_id=1, source_target_pairs={{2,0},{4,2},{6,4},{8,6},{10,8},{12,10},{14,12},{16,14},{18,16},{20... | collective-permute-start | bytes 3145736 | tf_op jit(solution)/shard_map/ppermute | solution.py:25
  218.1 8.4 %collective-permute-start.2 = (f32[2,1,512,256]{3,2,1,0:T(8,128)}, f32[2,1,512,256]{3,2,1,0:T(8,128)}, u32[]{:S(2)}, u32[]{:S(2)}) collective-permute-start(f32[2,1,512,256]{3,2,1,0:T(8,128)} %get-tuple-element.26), channel_id=1, source_target_pairs={{0,2},{2,4},{4,6},{6,8},{8,10},{10,12},{12,14},{14,16},{16,18},{18... | collective-permute-start | bytes 3145736 | tf_op jit(solution)/shard_map/ppermute | solution.py:23
  237.9 60.6 %copy-start.1 = (f32[18,2,32,256]{3,2,1,0:T(8,128)S(1)}, f32[18,2,32,256]{3,2,1,0:T(8,128)}, u32[]{:S(2)}) copy-start(f32[18,2,32,256]{3,2,1,0:T(8,128)} %param.10) | copy-start | bytes 3538948
  237.9 60.1 %copy-start.41 = (f32[2]{0:T(128)S(1)}, f32[2]{0:T(128)}, u32[]{:S(2)}) copy-start(f32[2]{0:T(128)} %constant.181) | copy-start | bytes 28
  (26 other events, 97.7 us)
Sparse Core Ops, SparseCore 0:
  15.4 154.8 all-gather.2
